TPU v7x, 256 devices: a whole 4x4x8 slice. The times are simulated.
256 devices in a mesh: view: 8 (over x, core), slab: 32 (over y, z).
Axes of the slice: x: 4, y: 4, z: 8, core: 2. Of those that a mesh axis runs over, the one named last changes fastest.
Arguments:
- image: float32 [128, 512, 512], P('slab'), may hold values from 0.1 to 10
- sensitivity: float32 [128, 512, 512], P('slab', 'view'), may hold values from 0.5 to 4
- resample_x: bfloat16 [16, 512, 512], P('view'), may hold values from 0 to 1, as said below
- resample_y: bfloat16 [16, 512, 512], P('view'), may hold values from 0 to 1, as said below
- tof_kernel: bfloat16 [16, 16, 512], P('view'), may hold values from 0.00019454956 to 0.0078125
- axial_mix: float32 [16, 128, 128], P('view'), may hold values from 0 to 1
- background: float32 [16, 16, 512, 128], P('view', None, 'slab'), may hold values from 0.5 to 2
- counts: int32 [16, 16, 512, 128], P('view', None, 'slab'), may hold values from 0 to 19
Outputs:
- new_image: float32 [128, 512, 512], P('slab', 'view')
Inputs may be any that keep to these rules, and one draw needn't show every extreme that they name: resample_x[v, a, x] is zero where |x - a| > 3. resample_y[v, y, b] is zero where |b - y| > 3.
All inputs are finite; a program needn't handle non-finite values.
Results may differ from a plain program's by a relative error of at most 0.00052.
Values may be sent and summed in bfloat16 or wider, within the bound.
A program may use at most 64 MiB of HBM per device.

v0:
```python
import jax
import jax.numpy as jnp
from jax import lax
from jax.sharding import PartitionSpec as P


def local(image, sensitivity, resample_x, resample_y, tof_kernel, axial_mix, background, counts):
    highest = lax.Precision.HIGHEST
    image_low = image.astype(jnp.bfloat16)
    along_y = jnp.einsum(
        "zxy,vyb->vzxb", image_low, resample_y, preferred_element_type=jnp.float32
    ).astype(jnp.bfloat16)
    rotated = jnp.einsum(
        "vzxb,vax->vzba", along_y, resample_x, preferred_element_type=jnp.float32
    ).astype(jnp.bfloat16)
    gathered = lax.all_to_all(rotated, "slab", split_axis=2, concat_axis=1, tiled=True)
    integrals = jnp.einsum(
        "vka,vzba->vkbz", tof_kernel, gathered, preferred_element_type=jnp.float32
    )
    expected = background + jnp.einsum("vkbz,vcz->vkbc", integrals, axial_mix, precision=highest)
    ratios = counts.astype(jnp.float32) / expected
    back_mixed = jnp.einsum("vkbc,vcz->vkbz", ratios, axial_mix, precision=highest).astype(
        jnp.bfloat16
    )
    spread = jnp.einsum(
        "vka,vkbz->vzba", tof_kernel, back_mixed, preferred_element_type=jnp.float32
    ).astype(jnp.bfloat16)
    frames = lax.all_to_all(spread, "slab", split_axis=1, concat_axis=2, tiled=True)
    unrotated = jnp.einsum(
        "vzba,vyb->vzya", frames, resample_y, preferred_element_type=jnp.float32
    ).astype(jnp.bfloat16)
    own_rows = image.shape[1] // lax.axis_size("view")
    gradient = lax.psum_scatter(
        jnp.einsum("vzya,vax->xzy", unrotated, resample_x, preferred_element_type=jnp.float32),
        "view",
        scatter_dimension=0,
        tiled=True,
    )
    gradient = jnp.transpose(gradient, (1, 0, 2))
    current = lax.dynamic_slice_in_dim(image, lax.axis_index("view") * own_rows, own_rows, 1)
    return current * gradient / sensitivity


def solution(mesh):
    in_specs = (
        P("slab", None, None),
        P("slab", "view", None),
        P("view", None, None),
        P("view", None, None),
        P("view", None, None),
        P("view", None, None),
        P("view", None, "slab", None),
        P("view", None, "slab", None),
    )
    out_specs = P("slab", "view", None)
    return jax.shard_map(local, mesh=mesh, in_specs=in_specs, out_specs=out_specs, check_vma=False)
```

profile of v0, /device:TPU:8, one launch (start us, length us, event | category | flops | bytes accessed | tf_op | source)
XLA Modules:
  0.0 340.9 jit_solution(16715669214694171133)
XLA Ops:
  6.5 0.0 copy-start
  6.5 0.0 all-reduce.3.cloned.1.call-start
  6.5 1.2 copy-done
  7.8 8.0 %fusion.8 = bf16[2,4,512,512]{3,2,1,0:T(8,128)(2,1)} fusion(f32[4,512,512]{2,1,0:T(8,128)} %param.8, bf16[2,512,512]{2,1,0:T(8,128)(2,1)S(1)} %copy-done, bf16[2,512,512]{2,1,0:T(8,128)(2,1)} %param.10), kind=kOutput, calls=%fused_computation.9 | convolution fusion | flops 4300210176 | bytes 10485760 | tf_op jit(solution)/shard_map/vzxb,vax->vzba/dot_general | solution.py:13
  15.7 5.4 %copy.44 = bf16[2,4,512,512]{3,1,0,2:T(4,128)(2,1)S(1)} copy(bf16[2,4,512,512]{3,2,1,0:T(8,128)(2,1)} %fusion.8) | data formatting | bytes 8388608 | tf_op jit(solution)/shard_map/convert_element_type | solution.py:15
  21.1 105.1 %all_to_all.36 = bf16[2,4,512,512]{3,1,0,2:T(4,128)(2,1)S(1)} all-to-all(bf16[2,4,512,512]{3,1,0,2:T(4,128)(2,1)S(1)} %copy.44), channel_id=1, replica_groups=mesh['view'=8,'slab'=32] {'slab'}, dimensions={2} | all-to-all | bytes 8388608 | tf_op jit(solution)/shard_map/all_to_all | solution.py:16
  126.2 1.4 copy.45
  127.6 0.0 copy-start.3
  127.6 0.6 copy.46
  128.3 0.1 copy-done.3
  128.4 0.0 copy-start.2
  128.4 1.2 convolution_bitcast_fusion
  129.6 0.8 copy.47
  130.5 0.0 copy-done.2
  130.5 1.4 fusion.24
  131.9 0.4 convolution_convert_fusion
  132.4 2.0 convert_bitcast_fusion
  134.4 2.4 copy.49
  136.8 100.6 %all_to_all.37 = bf16[2,128,16,512]{3,2,0,1:T(8,128)(2,1)S(1)} all-to-all(bf16[2,128,16,512]{3,2,0,1:T(8,128)(2,1)S(1)} %copy.49), channel_id=1, replica_groups=mesh['view'=8,'slab'=32] {'slab'}, dimensions={1} | all-to-all | bytes 8388608 | tf_op jit(solution)/shard_map/all_to_all | solution.py:28
  237.4 0.0 copy-start.4
  237.4 2.4 copy.51
  239.9 0.0 copy-done.4
  239.9 9.2 %fusion.13 = f32[512,4,512]{0,2,1:T(8,128)} fusion(bf16[2,4,512,512]{3,2,1,0:T(8,128)(2,1)} %bitcast.73, bf16[2,512,512]{2,1,0:T(8,128)(2,1)S(1)} %copy-done.4, bf16[2,512,512]{2,1,0:T(8,128)(2,1)S(1)} %copy-done), kind=kOutput, calls=%fused_computation.11 | convolution fusion | flops 4297064448 | bytes 10485760 | tf_op jit(solution)/shard_map/vzya,vax->xzy/dot_general | solution.py:34
  249.1 5.5 %copy.54 = f32[512,4,512]{2,1,0:T(4,128)} copy(f32[512,4,512]{0,2,1:T(8,128)} %fusion.13) | data formatting | bytes 8388608 | tf_op jit(solution)/shard_map/vzya,vax->xzy/dot_general | solution.py:34
  254.5 0.0 copy-start.5
  254.6 0.0 copy-start.1
  254.6 0.0 all-reduce.3.cloned.1.call-update
  254.6 0.6 copy-done.5
  255.2 0.6 dynamic-slice
  256.5 74.4 %all-reduce.3.cloned.1.call-done = f32[512,4,512]{2,1,0:T(4,128)} async-done(((f32[512,4,512]{2,1,0:T(4,128)}), f32[512,4,512]{2,1,0:T(4,128)}) %all-reduce.3.cloned.1.call-update) | async-done | bytes 4194320
  330.9 1.1 constant_dynamic-slice_fusion
  331.9 0.0 copy-done.1
  332.0 2.1 fusion.31
Async XLA Ops:
  6.5 1.2 copy-start
  6.5 324.3 %all-reduce.3.cloned.1.call-start = ((), (), s32[]{:S(2)}) async-start(), calls=%async_computation.2 | async-start | bytes 8388608
  127.6 0.8 copy-start.3
  128.4 2.1 copy-start.2
  237.4 2.5 copy-start.4
  254.5 0.7 copy-start.5
  254.6 77.4 %copy-start.1 = (f32[4,64,512]{2,1,0:T(8,128)S(1)}, f32[4,64,512]{2,1,0:T(8,128)}, u32[]{:S(2)}) copy-start(f32[4,64,512]{2,1,0:T(8,128)} %param.9) | copy-start | bytes 1572868
Sparse Core Ops, SparseCore 0:
  254.7 76.1 all-reduce.2
where the time goes:
time: 341 us
  blocking collectives  206 us (60%)
  waiting for transfers between devices  74.4 us (22%)
  local copies, waits for them, and re-layouts  22.3 us (7%)
  matrix products  22.3 us (7%)
  between operations  14.1 us (4%)
    all_to_all x1, blocking collectives, local(): lax.all_to_all(rotated, 'slab', split_axis=2, concat_axis=1, tiled=True)  105 us
    all_to_all x1, blocking collectives, local(): lax.all_to_all(spread, 'slab', split_axis=1, concat_axis=2, tiled=True)  101 us
    unnamed x2, waiting for transfers between devices  74.4 us
    dot_general x1, matrix products, local(): jnp.einsum('vzya,vax->xzy', unrotated, resample_x, preferred_element_type...  9.19 us
    dot_general x1, matrix products, local(): jnp.einsum('vzxb,vax->vzba', along_y, resample_x, preferred_element_type=...  7.96 us
  transfers between devices with their start and end apart: 1, of which 1 were waited for; matrix products, arithmetic and copies ran while one was open for 0% of the time, Pallas kernels for 0%

commit v1 on v0

--- a/solution.py
+++ b/solution.py
@@ -13,7 +13,10 @@
     rotated = jnp.einsum(
         "vzxb,vax->vzba", along_y, resample_x, preferred_element_type=jnp.float32
     ).astype(jnp.bfloat16)
-    gathered = lax.all_to_all(rotated, "slab", split_axis=2, concat_axis=1, tiled=True)
+    gathered = jnp.concatenate(
+        lax.all_to_all(jnp.stack(jnp.split(rotated, lax.axis_size("slab"), axis=2)), "slab", 0, 0),
+        axis=1,
+    )
     integrals = jnp.einsum(
         "vka,vzba->vkbz", tof_kernel, gathered, preferred_element_type=jnp.float32
     )

time: 341 us -> 365 us (1.070)
  local copies, waits for them, and re-layouts: 22.3 us -> 44.9 us
    unnamed x14 -> x45, local copies, waits for them, and re-layouts: 3.64 us -> 32.1 us
    convert_element_type x1 -> x0, local copies, waits for them, and re-layouts: 5.42 us -> none  [local(): rotated = jnp.einsum('vzxb,vax->vzba', along_y, resample_x, preferred_ele...]
where the time goes in v1:
time: 365 us; the launch traced here: 364 us
  blocking collectives  206 us (56%)
  waiting for transfers between devices  74.6 us (20%)
  local copies, waits for them, and re-layouts  44.9 us (12%)
  matrix products  22.3 us (6%)
  between operations  14.2 us (4%)
    all_to_all x1, blocking collectives, local(): lax.all_to_all(jnp.stack(jnp.split(rotated, lax.axis_size('slab'), axis=2...  105 us
    all_to_all x1, blocking collectives, local(): lax.all_to_all(spread, 'slab', split_axis=1, concat_axis=2, tiled=True)  101 us
    unnamed x2, waiting for transfers between devices  74.6 us
    unnamed x45, local copies, waits for them, and re-layouts  32.1 us
    dot_general x1, matrix products, local(): jnp.einsum('vzya,vax->xzy', unrotated, resample_x, preferred_element_type...  9.19 us
    dot_general x1, matrix products, local(): jnp.einsum('vzxb,vax->vzba', along_y, resample_x, preferred_element_type=...  7.96 us
  transfers between devices with their start and end apart: 1, of which 1 were waited for; matrix products, arithmetic and copies ran while one was open for 0% of the time, Pallas kernels for 0%

profile of v1, /device:TPU:8, one launch (start us, length us, event | category | flops | bytes accessed | tf_op | source)
XLA Modules:
  0.0 363.8 jit_solution(4648365904659545570)
XLA Ops:
  6.5 0.0 copy-start
  6.5 0.0 all-reduce.3.cloned.1.call-start
  6.5 1.2 copy-done
  7.8 8.0 %fusion.8 = bf16[2,4,512,512]{3,2,1,0:T(8,128)(2,1)} fusion(f32[4,512,512]{2,1,0:T(8,128)} %param.8, bf16[2,512,512]{2,1,0:T(8,128)(2,1)S(1)} %copy-done, bf16[2,512,512]{2,1,0:T(8,128)(2,1)} %param.10), kind=kOutput, calls=%fused_computation.9 | convolution fusion | flops 4300210176 | bytes 10485760 | tf_op jit(solution)/shard_map/vzxb,vax->vzba/dot_general | solution.py:13
  15.7 0.9 fusion.64
  16.6 0.9 fusion.63
  17.6 0.9 fusion.62
  18.5 0.9 fusion.61
  19.4 0.9 fusion.60
  20.3 0.9 fusion.59
  21.3 0.9 fusion.58
  22.2 0.9 fusion.57
  23.1 0.9 fusion.56
  24.0 0.9 fusion.55
  24.9 0.9 fusion.54
  25.9 0.9 fusion.53
  26.8 0.9 fusion.52
  27.7 0.9 fusion.51
  28.6 0.9 fusion.50
  29.6 0.9 fusion.49
  30.5 0.9 fusion.48
  31.4 0.9 fusion.47
  32.3 0.9 fusion.46
  33.3 0.9 fusion.45
  34.2 0.9 fusion.44
  35.1 0.9 fusion.43
  36.0 0.9 fusion.42
  36.9 0.9 fusion.41
  37.9 0.9 fusion.40
  38.8 0.9 fusion.39
  39.7 0.9 fusion.38
  40.6 0.9 fusion.37
  41.6 0.9 fusion.36
  42.5 0.9 fusion.35
  43.4 0.9 fusion.34
  44.3 0.9 fusion.33
  45.3 105.0 %all_to_all.23 = bf16[32,2,4,16,512]{4,3,2,1,0:T(8,128)(2,1)S(1)} all-to-all(bf16[32,2,4,16,512]{4,3,2,1,0:T(8,128)(2,1)S(1)} %fusion.33), channel_id=1, replica_groups=mesh['view'=8,'slab'=32] {'slab'}, dimensions={0} | all-to-all | bytes 8388608 | tf_op jit(solution)/shard_map/all_to_all | solution.py:17
  150.2 0.0 copy-start.3
  150.2 0.8 copy.42
  151.1 0.0 copy-done.3
  151.1 0.0 copy-start.2
  151.1 1.2 convolution_bitcast_fusion
  152.3 0.8 copy.43
  153.1 0.0 copy-done.2
  153.1 1.4 fusion.24
  154.6 0.4 convolution_convert_fusion
  155.0 2.0 convert_bitcast_fusion
  157.1 2.4 copy.45
  159.5 100.6 %all_to_all.24 = bf16[2,128,16,512]{3,2,0,1:T(8,128)(2,1)S(1)} all-to-all(bf16[2,128,16,512]{3,2,0,1:T(8,128)(2,1)S(1)} %copy.45), channel_id=1, replica_groups=mesh['view'=8,'slab'=32] {'slab'}, dimensions={1} | all-to-all | bytes 8388608 | tf_op jit(solution)/shard_map/all_to_all | solution.py:31
  260.1 0.0 copy-start.4
  260.1 2.4 copy.47
  262.6 0.0 copy-done.4
  262.6 9.2 %fusion.13 = f32[512,4,512]{0,2,1:T(8,128)} fusion(bf16[2,4,512,512]{3,2,1,0:T(8,128)(2,1)} %bitcast.199, bf16[2,512,512]{2,1,0:T(8,128)(2,1)S(1)} %copy-done.4, bf16[2,512,512]{2,1,0:T(8,128)(2,1)S(1)} %copy-done), kind=kOutput, calls=%fused_computation.11 | convolution fusion | flops 4297064448 | bytes 10485760 | tf_op jit(solution)/shard_map/vzya,vax->xzy/dot_general | solution.py:37
  271.8 5.5 %copy.50 = f32[512,4,512]{2,1,0:T(4,128)} copy(f32[512,4,512]{0,2,1:T(8,128)} %fusion.13) | data formatting | bytes 8388608 | tf_op jit(solution)/shard_map/vzya,vax->xzy/dot_general | solution.py:37
  277.2 0.0 copy-start.5
  277.2 0.0 copy-start.1
  277.2 0.0 all-reduce.3.cloned.1.call-update
  277.3 0.6 copy-done.5
  277.9 0.6 dynamic-slice
  279.2 74.6 %all-reduce.3.cloned.1.call-done = f32[512,4,512]{2,1,0:T(4,128)} async-done(((f32[512,4,512]{2,1,0:T(4,128)}), f32[512,4,512]{2,1,0:T(4,128)}) %all-reduce.3.cloned.1.call-update) | async-done | bytes 4194320
  353.7 1.1 constant_dynamic-slice_fusion
  354.8 0.0 copy-done.1
  354.8 2.1 fusion.31
Async XLA Ops:
  6.5 1.2 copy-start
  6.5 347.2 %all-reduce.3.cloned.1.call-start = ((), (), s32[]{:S(2)}) async-start(), calls=%async_computation.2 | async-start | bytes 8388608
  150.2 0.8 copy-start.3
  151.1 2.1 copy-start.2
  260.1 2.5 copy-start.4
  277.2 0.7 copy-start.5
  277.2 77.6 %copy-start.1 = (f32[4,64,512]{2,1,0:T(8,128)S(1)}, f32[4,64,512]{2,1,0:T(8,128)}, u32[]{:S(2)}) copy-start(f32[4,64,512]{2,1,0:T(8,128)} %param.9) | copy-start | bytes 1572868
Sparse Core Ops, SparseCore 0:
  277.4 76.2 all-reduce.2
